TPU v7x, 32 devices: a whole 2x2x4 slice. The times are simulated.
32 devices in a mesh: groups: 2 (over y), track: 4 (over z), across: 2 (over x), disp: 2 (over core).
Axes of the slice: x: 2, y: 2, z: 4, core: 2. Of those that a mesh axis runs over, the one named last changes fastest.
Arguments:
- ref_image: bfloat16 [128, 512], P(('groups', 'across'), 'track'), parts along dimension 0, may hold values from -8 to 8
- source_one: bfloat16 [128, 512], P(('groups', 'across'), 'track'), parts along dimension 0, may hold values from -8 to 8
- source_two: bfloat16 [128, 512], P(('groups', 'across'), 'track'), parts along dimension 0, may hold values from -8 to 8
- plane_offsets: int32 [256], P('disp'), may hold values from 0 to 319, as said below
- intersection_mask: int32 [2, 4, 4], P(None, ('groups', 'across'), 'track'), parts along dimension 1, may hold values 0 or 1
Outputs:
- disparity_map: float32 [128, 512], P(('groups', 'across'), 'track'), parts along dimension 0
- soft_cost: float32 [128, 512], P(('groups', 'across'), 'track'), parts along dimension 0
There are 2 independent parts, one for each index of `groups`. A program takes and returns all parts, laid end to end along the dimension named above; an argument that names none is the same for every part. Nothing has to cross between parts.
Inputs may be any that keep to these rules, and one draw needn't show every extreme that they name: `plane_offsets`: distinct and increasing; the first is 0 and the last is 319.
All inputs are finite; a program needn't handle non-finite values. No bound on the sum of `intersection_mask` on one device may be relied on, other than what follows from the above.
Results may differ from a plain program's by a relative error of at most 0.0003.
Values may be sent and summed in bfloat16 or wider, within the bound.
A program may use at most 64 MiB of HBM per device.

v0:
```python
import jax
import jax.numpy as jnp
from jax import lax
from jax.sharding import PartitionSpec as P

MAXD = 320
RADIUS = 15


clip_level = 2.0
exponent_sharpness = 0.005
disparity_interval = 64.0
highest_precision = lax.Precision.HIGHEST


def shifted_2(value, axis, steps):
    count = lax.axis_size(axis)
    leading, last = (max(0, -steps), min(count, count - steps))
    return lax.ppermute(value, axis, [(source, source + steps) for source in range(leading, last)])


def extended_2(value, sides, width):
    for axis, dim in sides:
        size, length = (lax.axis_size(axis), value.shape[dim])
        up = [(i, (i + 1) % size) for i in range(size - 1)]
        down = [(j, i) for i, j in up]
        last = lax.slice_in_dim(value, length - width, length, axis=dim)
        leading = lax.slice_in_dim(value, 0, width, axis=dim)
        before = lax.ppermute(last, axis, up)
        after = lax.ppermute(leading, axis, down)
        value = jnp.concatenate([before, value, after], axis=dim)
    return value


def band_matrix(extended, narrow):
    outer = lax.broadcasted_iota(jnp.int32, (extended, narrow), 0)
    inner = lax.broadcasted_iota(jnp.int32, (extended, narrow), 1)
    distance = outer - inner
    return ((distance >= 0) & (distance <= 2 * RADIUS)).astype(jnp.float32)


def window_count(position, length):
    upper_part = jnp.minimum(position + RADIUS, length - 1)
    lower_part = jnp.maximum(position - RADIUS, 0)
    return (upper_part - lower_part + 1).astype(jnp.float32)


def earlier_tiles(own_tiles, tiles_back):
    pieces = [own_tiles]
    current = own_tiles
    for step_back in range(tiles_back):
        current = shifted_2(current, "track", 1)
        pieces.insert(0, current)
    return jnp.concatenate(pieces, axis=2)


def shards(ref_image, source_one, source_two, plane_offsets, intersection_mask):
    tile_cols, tile_rows = ref_image.shape
    track_devices = lax.axis_size("track")
    total_rows = tile_rows * track_devices
    total_cols = tile_cols * lax.axis_size("across")
    row_base = lax.axis_index("track") * tile_rows
    col_base = lax.axis_index("across") * tile_cols
    tiles_back = (2 * (MAXD - 1) + RADIUS + tile_rows - 1) // tile_rows
    stacked = jnp.stack([ref_image, source_one, source_two])
    rimmed = extended_2(stacked, (("track", 2), ("across", 1)), RADIUS)
    own_tiles = rimmed[1:, :, RADIUS : RADIUS + tile_rows]
    ahead = rimmed[1:, :, RADIUS + tile_rows :]
    window = jnp.concatenate([earlier_tiles(own_tiles, tiles_back), ahead], axis=2)
    reference_part = rimmed[0].astype(jnp.float32)
    first_row = row_base - RADIUS
    first_col = col_base - RADIUS
    part_cols, part_rows = reference_part.shape
    window_rows = window.shape[2]
    window_start = row_base - tiles_back * tile_rows
    grid_rows = first_row + jnp.arange(part_rows, dtype=jnp.int32)
    grid_cols = first_col + jnp.arange(part_cols, dtype=jnp.int32)
    inside = ((grid_cols >= 0) & (grid_cols < total_cols))[:, None] & (
        (grid_rows >= 0) & (grid_rows < total_rows)
    )[None, :]
    window_index = lax.broadcasted_iota(jnp.int32, (1, window_rows, part_rows), 1)
    target_index = lax.broadcasted_iota(jnp.int32, (1, window_rows, part_rows), 2)

    def frame_block(offsets, frame_index):
        shifted = (frame_index + 1) * offsets
        begin = first_row - window_start - shifted
        selector = (window_index == target_index + begin[:, None, None]).astype(jnp.bfloat16)
        sampled = jnp.einsum(
            "cu,qut->qct", window[frame_index], selector, preferred_element_type=jnp.float32
        )
        usable = grid_rows[None, :] - shifted[:, None] >= 0
        clipped = jnp.minimum(jnp.abs(reference_part[None] - sampled), clip_level)
        return jnp.where(
            usable[:, None, :] & inside[None], clipped, jnp.where(inside[None], clip_level, 0.0)
        )

    row_band = band_matrix(tile_rows + 2 * RADIUS, tile_rows)
    col_band = band_matrix(tile_cols + 2 * RADIUS, tile_cols)
    own_rows = row_base + jnp.arange(tile_rows, dtype=jnp.int32)
    own_cols = col_base + jnp.arange(tile_cols, dtype=jnp.int32)
    cell_count = (
        window_count(own_cols, total_cols)[:, None] * window_count(own_rows, total_rows)[None, :]
    )
    masks = intersection_mask[:, 0, 0].astype(jnp.float32)
    mask_total = jnp.maximum(masks[0] + masks[1], 1.0)

    def aggregate(terms):
        along_rows = jnp.einsum("qcu,ut->qct", terms, row_band, precision=highest_precision)
        return jnp.einsum("qct,cd->qdt", along_rows, col_band, precision=highest_precision)

    planes_here = plane_offsets.shape[0]
    block = min(16, planes_here)
    offset_blocks = plane_offsets.reshape(planes_here // block, block)

    def block_step(running, offsets):
        highest_seen, normalizer_mass, disparity_moment_accumulator = running
        terms = jnp.concatenate([frame_block(offsets, 0), frame_block(offsets, 1)], axis=0)
        summed = aggregate(terms)
        means = summed / cell_count
        hypothesis_matching_penalty = (
            masks[0] * means[:block] + masks[1] * means[block:]
        ) / mask_total
        hypothesis_likelihoods = -hypothesis_matching_penalty / exponent_sharpness
        new_top = jnp.maximum(highest_seen, jnp.max(hypothesis_likelihoods, axis=0))
        fading = jnp.exp(highest_seen - new_top)
        lifted = jnp.exp(hypothesis_likelihoods - new_top)
        plane_values = offsets.astype(jnp.float32)[:, None, None]
        return (
            (
                new_top,
                normalizer_mass * fading + jnp.sum(lifted, axis=0),
                disparity_moment_accumulator * fading + jnp.sum(lifted * plane_values, axis=0),
            ),
            None,
        )

    initial = jnp.full((tile_cols, tile_rows), -jnp.inf, jnp.float32)
    blank_map = jnp.zeros((tile_cols, tile_rows), jnp.float32)
    (highest_seen, normalizer_mass, disparity_moment_accumulator), _ = lax.scan(
        block_step, (initial, blank_map, blank_map), offset_blocks
    )
    global_maximal_likelihood = lax.pmax(highest_seen, "disp")
    fading = jnp.exp(highest_seen - global_maximal_likelihood)
    normalizer_mass, disparity_moment_accumulator = lax.psum(
        (normalizer_mass * fading, disparity_moment_accumulator * fading), "disp"
    )
    return (
        disparity_moment_accumulator / normalizer_mass / disparity_interval,
        -exponent_sharpness * (global_maximal_likelihood + jnp.log(normalizer_mass)),
    )


def solution(mesh):
    in_specs = (
        P(("groups", "across"), "track"),
        P(("groups", "across"), "track"),
        P(("groups", "across"), "track"),
        P("disp"),
        P(None, ("groups", "across"), "track"),
    )
    out_specs = (P(("groups", "across"), "track"), P(("groups", "across"), "track"))
    return jax.shard_map(shards, mesh=mesh, in_specs=in_specs, out_specs=out_specs, check_vma=False)
```

profile of v0, /device:TPU:0, one launch (start us, length us, event | category | flops | bytes accessed | tf_op | source)
XLA Modules:
  0.0 209.6 jit_solution(3467940691298570824)
XLA Ops:
  1.4 4.9 %collective-permute-start = (bf16[3,32,15]{2,1,0:T(8,128)(2,1)S(1)}, bf16[3,32,15]{2,1,0:T(8,128)(2,1)S(1)}, u32[]{:S(2)}, u32[]{:S(2)}) collective-permute-start(bf16[3,32,15]{2,1,0:T(8,128)(2,1)S(1)} %get-tuple-element.375), channel_id=1, source_target_pairs={{0,4},{4,8},{8,12},{1,5},{5,9},{9,13},{2,6},{6,10},{10,14},{3,7},{... | collective-permute-start | bytes 8648 | tf_op jit(solution)/shard_map/ppermute | solution.py:29
  6.4 1.3 collective-permute-start.1
  7.9 4.2 %collective-permute-done.1 = bf16[3,32,15]{2,1,0:T(8,128)(2,1)S(1)} collective-permute-done((bf16[3,32,15]{2,1,0:T(8,128)(2,1)S(1)}, bf16[3,32,15]{2,1,0:T(8,128)(2,1)S(1)}, u32[]{:S(2)}, u32[]{:S(2)}) %collective-permute-start.1) | collective-permute-done | bytes 2912 | tf_op jit(solution)/shard_map/ppermute | solution.py:30
  12.1 0.8 pad_maximum_fusion.1
  13.0 3.4 %collective-permute-start.2 = (bf16[3,15,158]{2,1,0:T(8,128)(2,1)S(1)}, bf16[3,15,158]{2,1,0:T(8,128)(2,1)S(1)}, u32[]{:S(2)}, u32[]{:S(2)}) collective-permute-start(bf16[3,15,158]{2,1,0:T(8,128)(2,1)S(1)} %get-tuple-element.371), channel_id=1, source_target_pairs={{0,2},{1,3},{4,6},{5,7},{8,10},{9,11},{12,14},{13,15},{16,18},{17,... | collective-permute-start | bytes 42668 | tf_op jit(solution)/shard_map/ppermute | solution.py:29
  16.4 1.3 collective-permute-start.3
  18.3 3.8 %collective-permute-done.3 = bf16[3,15,158]{2,1,0:T(8,128)(2,1)S(1)} collective-permute-done((bf16[3,15,158]{2,1,0:T(8,128)(2,1)S(1)}, bf16[3,15,158]{2,1,0:T(8,128)(2,1)S(1)}, u32[]{:S(2)}, u32[]{:S(2)}) %collective-permute-start.3) | collective-permute-done | bytes 14252 | tf_op jit(solution)/shard_map/ppermute | solution.py:30
  22.1 0.8 pad_maximum_fusion
  23.0 3.5 %collective-permute-start.4 = (bf16[2,62,128]{2,1,0:T(8,128)(2,1)S(1)}, bf16[2,62,128]{2,1,0:T(8,128)(2,1)S(1)}, u32[]{:S(2)}, u32[]{:S(2)}) collective-permute-start(bf16[2,62,128]{2,1,0:T(8,128)(2,1)S(1)} %slice.88), channel_id=1, source_target_pairs={{0,4},{4,8},{8,12},{1,5},{5,9},{9,13},{2,6},{6,10},{10,14},{3,7},{... | collective-permute-start | bytes 95240 | tf_op jit(solution)/shard_map/ppermute | solution.py:19
  27.1 1.0 collective-permute-done.4
  28.1 4.2 %collective-permute-start.5 = (bf16[2,62,128]{2,1,0:T(8,128)(2,1)S(1)}, bf16[2,62,128]{2,1,0:T(8,128)(2,1)S(1)}, u32[]{:S(2)}, u32[]{:S(2)}) collective-permute-start(bf16[2,62,128]{2,1,0:T(8,128)(2,1)S(1)} %collective-permute-done.4), channel_id=1, source_target_pairs={{0,4},{4,8},{8,12},{1,5},{5,9},{9,13},{2,6},{6,10},{10,14},{3,7},{... | collective-permute-start | bytes 95240 | tf_op jit(solution)/shard_map/ppermute | solution.py:19
  32.3 1.6 collective-permute-done.5
  33.9 4.2 %collective-permute-start.6 = (bf16[2,62,128]{2,1,0:T(8,128)(2,1)S(1)}, bf16[2,62,128]{2,1,0:T(8,128)(2,1)S(1)}, u32[]{:S(2)}, u32[]{:S(2)}) collective-permute-start(bf16[2,62,128]{2,1,0:T(8,128)(2,1)S(1)} %collective-permute-done.5), channel_id=1, source_target_pairs={{0,4},{4,8},{8,12},{1,5},{5,9},{9,13},{2,6},{6,10},{10,14},{3,7},{... | collective-permute-start | bytes 95240 | tf_op jit(solution)/shard_map/ppermute | solution.py:19
  38.1 1.6 collective-permute-done.6
  39.7 4.2 %collective-permute-start.7 = (bf16[2,62,128]{2,1,0:T(8,128)(2,1)S(1)}, bf16[2,62,128]{2,1,0:T(8,128)(2,1)S(1)}, u32[]{:S(2)}, u32[]{:S(2)}) collective-permute-start(bf16[2,62,128]{2,1,0:T(8,128)(2,1)S(1)} %collective-permute-done.6), channel_id=1, source_target_pairs={{0,4},{4,8},{8,12},{1,5},{5,9},{9,13},{2,6},{6,10},{10,14},{3,7},{... | collective-permute-start | bytes 95240 | tf_op jit(solution)/shard_map/ppermute | solution.py:19
  43.9 1.6 collective-permute-done.7
  45.5 4.2 %collective-permute-start.8 = (bf16[2,62,128]{2,1,0:T(8,128)(2,1)S(1)}, bf16[2,62,128]{2,1,0:T(8,128)(2,1)S(1)}, u32[]{:S(2)}, u32[]{:S(2)}) collective-permute-start(bf16[2,62,128]{2,1,0:T(8,128)(2,1)S(1)} %collective-permute-done.7), channel_id=1, source_target_pairs={{0,4},{4,8},{8,12},{1,5},{5,9},{9,13},{2,6},{6,10},{10,14},{3,7},{... | collective-permute-start | bytes 95240 | tf_op jit(solution)/shard_map/ppermute | solution.py:19
  51.7 3.8 %collective-permute-start.9 = (bf16[2,62,128]{2,1,0:T(8,128)(2,1)S(1)}, bf16[2,62,128]{2,1,0:T(8,128)(2,1)S(1)}, u32[]{:S(2)}, u32[]{:S(2)}) collective-permute-start(bf16[2,62,128]{2,1,0:T(8,128)(2,1)S(1)} %collective-permute-done.8), channel_id=1, source_target_pairs={{0,4},{4,8},{8,12},{1,5},{5,9},{9,13},{2,6},{6,10},{10,14},{3,7},{... | collective-permute-start | bytes 95240 | tf_op jit(solution)/shard_map/ppermute | solution.py:19
  55.5 1.6 collective-permute-done.9
  57.3 144.7 %while.18 = (s32[]{:T(128)}, f32[32,128]{1,0:T(8,128)S(1)}, f32[32,128]{1,0:T(8,128)S(1)}, f32[32,128]{1,0:T(8,128)S(1)}, f32[2]{0:T(128)S(1)}, /*index=5*/s32[8...) while((s32[]{:T(128)}, f32[32,128]{1,0:T(8,128)S(1)}, ...), condition=%wide.region_4.5_spmd.clone.clone, body=%wide.region_0.4_spmd.clone.clone.sunk | while | flops 1162284800 | bytes 16829516 | solution.py:139
  57.3 4.8 %iota_compare_fusion.3 = (pred[16,911,158]{1,0,2:T(8,128)(4,1)S(1)}, pred[16,911,158]{1,0,2:T(8,128)(4,1)S(1)}) fusion(s32[16]{0:T(128)S(1)} %get-tuple-element.492, s32[16]{0:T(128)S(1)} %get-tuple-element.493), kind=kLoop, calls=%fused_computation.9.clone.1 | loop fusion | flops 9212032 | bytes 4606144 | tf_op jit(solution)/shard_map/while/body/eval_jaxpr/eq | solution.py:87
  62.4 4.1 %fusion.125 = f32[16,62,158]{2,1,0:T(8,128)S(1)} fusion(pred[16,911,158]{1,0,2:T(8,128)(4,1)S(1)} %get-tuple-element.497, f32[62,158]{1,0:T(8,128)S(1)} %broadcast_select_fusion.2, f32[62,158]{1,0:T(8,128)S(1)} %get-tuple-element.548, pred[62,158]{1,0:T(8,128)(4,1)S(1)} %broadcast_and_fusion.2, pred[16,158]{1,0:T(8,128)(4,1)S(1)} %get-tuple-element.498, ...), kind=kOutput, calls=%fused_computation.27.clone.1 | convolution fusion | flops 286356672 | bytes 3498240 | tf_op jit(solution)/shard_map/while/body/eval_jaxpr/cu,qut->qct/dot_general | solution.py:88
  66.5 4.1 %fusion.124 = f32[16,62,158]{2,1,0:T(8,128)S(1)} fusion(pred[16,911,158]{1,0,2:T(8,128)(4,1)S(1)} %get-tuple-element.494, f32[62,158]{1,0:T(8,128)S(1)} %broadcast_select_fusion.2, f32[62,158]{1,0:T(8,128)S(1)} %get-tuple-element.548, pred[16,158]{1,0:T(8,128)(4,1)S(1)} %get-tuple-element.496, pred[62,158]{1,0:T(8,128)(4,1)S(1)} %broadcast_and_fusion.2, ...), kind=kOutput, calls=%fused_computation.28.clone.1 | convolution fusion | flops 286356672 | bytes 3498240 | tf_op jit(solution)/shard_map/while/body/eval_jaxpr/cu,qut->qct/dot_general | solution.py:88
  70.6 1.8 fusion.126
  73.9 1.3 fusion.129
  75.4 4.8 %iota_compare_fusion.3 = (pred[16,911,158]{1,0,2:T(8,128)(4,1)S(1)}, pred[16,911,158]{1,0,2:T(8,128)(4,1)S(1)}) fusion(s32[16]{0:T(128)S(1)} %get-tuple-element.492, s32[16]{0:T(128)S(1)} %get-tuple-element.493), kind=kLoop, calls=%fused_computation.9.clone.1 | loop fusion | flops 9212032 | bytes 4606144 | tf_op jit(solution)/shard_map/while/body/eval_jaxpr/eq | solution.py:87
  80.5 4.1 %fusion.125 = f32[16,62,158]{2,1,0:T(8,128)S(1)} fusion(pred[16,911,158]{1,0,2:T(8,128)(4,1)S(1)} %get-tuple-element.497, f32[62,158]{1,0:T(8,128)S(1)} %broadcast_select_fusion.2, f32[62,158]{1,0:T(8,128)S(1)} %get-tuple-element.548, pred[62,158]{1,0:T(8,128)(4,1)S(1)} %broadcast_and_fusion.2, pred[16,158]{1,0:T(8,128)(4,1)S(1)} %get-tuple-element.498, ...), kind=kOutput, calls=%fused_computation.27.clone.1 | convolution fusion | flops 286356672 | bytes 3498240 | tf_op jit(solution)/shard_map/while/body/eval_jaxpr/cu,qut->qct/dot_general | solution.py:88
  84.6 4.1 %fusion.124 = f32[16,62,158]{2,1,0:T(8,128)S(1)} fusion(pred[16,911,158]{1,0,2:T(8,128)(4,1)S(1)} %get-tuple-element.494, f32[62,158]{1,0:T(8,128)S(1)} %broadcast_select_fusion.2, f32[62,158]{1,0:T(8,128)S(1)} %get-tuple-element.548, pred[16,158]{1,0:T(8,128)(4,1)S(1)} %get-tuple-element.496, pred[62,158]{1,0:T(8,128)(4,1)S(1)} %broadcast_and_fusion.2, ...), kind=kOutput, calls=%fused_computation.28.clone.1 | convolution fusion | flops 286356672 | bytes 3498240 | tf_op jit(solution)/shard_map/while/body/eval_jaxpr/cu,qut->qct/dot_general | solution.py:88
  88.7 1.8 fusion.126
  92.0 1.3 fusion.129
  93.5 4.8 %iota_compare_fusion.3 = (pred[16,911,158]{1,0,2:T(8,128)(4,1)S(1)}, pred[16,911,158]{1,0,2:T(8,128)(4,1)S(1)}) fusion(s32[16]{0:T(128)S(1)} %get-tuple-element.492, s32[16]{0:T(128)S(1)} %get-tuple-element.493), kind=kLoop, calls=%fused_computation.9.clone.1 | loop fusion | flops 9212032 | bytes 4606144 | tf_op jit(solution)/shard_map/while/body/eval_jaxpr/eq | solution.py:87
  98.6 4.1 %fusion.125 = f32[16,62,158]{2,1,0:T(8,128)S(1)} fusion(pred[16,911,158]{1,0,2:T(8,128)(4,1)S(1)} %get-tuple-element.497, f32[62,158]{1,0:T(8,128)S(1)} %broadcast_select_fusion.2, f32[62,158]{1,0:T(8,128)S(1)} %get-tuple-element.548, pred[62,158]{1,0:T(8,128)(4,1)S(1)} %broadcast_and_fusion.2, pred[16,158]{1,0:T(8,128)(4,1)S(1)} %get-tuple-element.498, ...), kind=kOutput, calls=%fused_computation.27.clone.1 | convolution fusion | flops 286356672 | bytes 3498240 | tf_op jit(solution)/shard_map/while/body/eval_jaxpr/cu,qut->qct/dot_general | solution.py:88
  102.7 4.1 %fusion.124 = f32[16,62,158]{2,1,0:T(8,128)S(1)} fusion(pred[16,911,158]{1,0,2:T(8,128)(4,1)S(1)} %get-tuple-element.494, f32[62,158]{1,0:T(8,128)S(1)} %broadcast_select_fusion.2, f32[62,158]{1,0:T(8,128)S(1)} %get-tuple-element.548, pred[16,158]{1,0:T(8,128)(4,1)S(1)} %get-tuple-element.496, pred[62,158]{1,0:T(8,128)(4,1)S(1)} %broadcast_and_fusion.2, ...), kind=kOutput, calls=%fused_computation.28.clone.1 | convolution fusion | flops 286356672 | bytes 3498240 | tf_op jit(solution)/shard_map/while/body/eval_jaxpr/cu,qut->qct/dot_general | solution.py:88
  106.8 1.8 fusion.126
  108.7 0.8 fusion.127
  110.1 1.3 fusion.129
  111.6 4.8 %iota_compare_fusion.3 = (pred[16,911,158]{1,0,2:T(8,128)(4,1)S(1)}, pred[16,911,158]{1,0,2:T(8,128)(4,1)S(1)}) fusion(s32[16]{0:T(128)S(1)} %get-tuple-element.492, s32[16]{0:T(128)S(1)} %get-tuple-element.493), kind=kLoop, calls=%fused_computation.9.clone.1 | loop fusion | flops 9212032 | bytes 4606144 | tf_op jit(solution)/shard_map/while/body/eval_jaxpr/eq | solution.py:87
  116.7 4.1 %fusion.125 = f32[16,62,158]{2,1,0:T(8,128)S(1)} fusion(pred[16,911,158]{1,0,2:T(8,128)(4,1)S(1)} %get-tuple-element.497, f32[62,158]{1,0:T(8,128)S(1)} %broadcast_select_fusion.2, f32[62,158]{1,0:T(8,128)S(1)} %get-tuple-element.548, pred[62,158]{1,0:T(8,128)(4,1)S(1)} %broadcast_and_fusion.2, pred[16,158]{1,0:T(8,128)(4,1)S(1)} %get-tuple-element.498, ...), kind=kOutput, calls=%fused_computation.27.clone.1 | convolution fusion | flops 286356672 | bytes 3498240 | tf_op jit(solution)/shard_map/while/body/eval_jaxpr/cu,qut->qct/dot_general | solution.py:88
  120.8 4.1 %fusion.124 = f32[16,62,158]{2,1,0:T(8,128)S(1)} fusion(pred[16,911,158]{1,0,2:T(8,128)(4,1)S(1)} %get-tuple-element.494, f32[62,158]{1,0:T(8,128)S(1)} %broadcast_select_fusion.2, f32[62,158]{1,0:T(8,128)S(1)} %get-tuple-element.548, pred[16,158]{1,0:T(8,128)(4,1)S(1)} %get-tuple-element.496, pred[62,158]{1,0:T(8,128)(4,1)S(1)} %broadcast_and_fusion.2, ...), kind=kOutput, calls=%fused_computation.28.clone.1 | convolution fusion | flops 286356672 | bytes 3498240 | tf_op jit(solution)/shard_map/while/body/eval_jaxpr/cu,qut->qct/dot_general | solution.py:88
  124.9 1.8 fusion.126
  126.8 0.8 fusion.127
  128.2 1.3 fusion.129
  129.7 4.8 %iota_compare_fusion.3 = (pred[16,911,158]{1,0,2:T(8,128)(4,1)S(1)}, pred[16,911,158]{1,0,2:T(8,128)(4,1)S(1)}) fusion(s32[16]{0:T(128)S(1)} %get-tuple-element.492, s32[16]{0:T(128)S(1)} %get-tuple-element.493), kind=kLoop, calls=%fused_computation.9.clone.1 | loop fusion | flops 9212032 | bytes 4606144 | tf_op jit(solution)/shard_map/while/body/eval_jaxpr/eq | solution.py:87
  134.7 4.1 %fusion.125 = f32[16,62,158]{2,1,0:T(8,128)S(1)} fusion(pred[16,911,158]{1,0,2:T(8,128)(4,1)S(1)} %get-tuple-element.497, f32[62,158]{1,0:T(8,128)S(1)} %broadcast_select_fusion.2, f32[62,158]{1,0:T(8,128)S(1)} %get-tuple-element.548, pred[62,158]{1,0:T(8,128)(4,1)S(1)} %broadcast_and_fusion.2, pred[16,158]{1,0:T(8,128)(4,1)S(1)} %get-tuple-element.498, ...), kind=kOutput, calls=%fused_computation.27.clone.1 | convolution fusion | flops 286356672 | bytes 3498240 | tf_op jit(solution)/shard_map/while/body/eval_jaxpr/cu,qut->qct/dot_general | solution.py:88
  138.9 4.1 %fusion.124 = f32[16,62,158]{2,1,0:T(8,128)S(1)} fusion(pred[16,911,158]{1,0,2:T(8,128)(4,1)S(1)} %get-tuple-element.494, f32[62,158]{1,0:T(8,128)S(1)} %broadcast_select_fusion.2, f32[62,158]{1,0:T(8,128)S(1)} %get-tuple-element.548, pred[16,158]{1,0:T(8,128)(4,1)S(1)} %get-tuple-element.496, pred[62,158]{1,0:T(8,128)(4,1)S(1)} %broadcast_and_fusion.2, ...), kind=kOutput, calls=%fused_computation.28.clone.1 | convolution fusion | flops 286356672 | bytes 3498240 | tf_op jit(solution)/shard_map/while/body/eval_jaxpr/cu,qut->qct/dot_general | solution.py:88
  143.0 1.8 fusion.126
  146.3 1.3 fusion.129
  147.7 4.8 %iota_compare_fusion.3 = (pred[16,911,158]{1,0,2:T(8,128)(4,1)S(1)}, pred[16,911,158]{1,0,2:T(8,128)(4,1)S(1)}) fusion(s32[16]{0:T(128)S(1)} %get-tuple-element.492, s32[16]{0:T(128)S(1)} %get-tuple-element.493), kind=kLoop, calls=%fused_computation.9.clone.1 | loop fusion | flops 9212032 | bytes 4606144 | tf_op jit(solution)/shard_map/while/body/eval_jaxpr/eq | solution.py:87
  152.8 4.1 %fusion.125 = f32[16,62,158]{2,1,0:T(8,128)S(1)} fusion(pred[16,911,158]{1,0,2:T(8,128)(4,1)S(1)} %get-tuple-element.497, f32[62,158]{1,0:T(8,128)S(1)} %broadcast_select_fusion.2, f32[62,158]{1,0:T(8,128)S(1)} %get-tuple-element.548, pred[62,158]{1,0:T(8,128)(4,1)S(1)} %broadcast_and_fusion.2, pred[16,158]{1,0:T(8,128)(4,1)S(1)} %get-tuple-element.498, ...), kind=kOutput, calls=%fused_computation.27.clone.1 | convolution fusion | flops 286356672 | bytes 3498240 | tf_op jit(solution)/shard_map/while/body/eval_jaxpr/cu,qut->qct/dot_general | solution.py:88
  157.0 4.1 %fusion.124 = f32[16,62,158]{2,1,0:T(8,128)S(1)} fusion(pred[16,911,158]{1,0,2:T(8,128)(4,1)S(1)} %get-tuple-element.494, f32[62,158]{1,0:T(8,128)S(1)} %broadcast_select_fusion.2, f32[62,158]{1,0:T(8,128)S(1)} %get-tuple-element.548, pred[16,158]{1,0:T(8,128)(4,1)S(1)} %get-tuple-element.496, pred[62,158]{1,0:T(8,128)(4,1)S(1)} %broadcast_and_fusion.2, ...), kind=kOutput, calls=%fused_computation.28.clone.1 | convolution fusion | flops 286356672 | bytes 3498240 | tf_op jit(solution)/shard_map/while/body/eval_jaxpr/cu,qut->qct/dot_general | solution.py:88
  161.1 1.8 fusion.126
  164.4 1.3 fusion.129
  165.8 4.8 %iota_compare_fusion.3 = (pred[16,911,158]{1,0,2:T(8,128)(4,1)S(1)}, pred[16,911,158]{1,0,2:T(8,128)(4,1)S(1)}) fusion(s32[16]{0:T(128)S(1)} %get-tuple-element.492, s32[16]{0:T(128)S(1)} %get-tuple-element.493), kind=kLoop, calls=%fused_computation.9.clone.1 | loop fusion | flops 9212032 | bytes 4606144 | tf_op jit(solution)/shard_map/while/body/eval_jaxpr/eq | solution.py:87
  170.9 4.1 %fusion.125 = f32[16,62,158]{2,1,0:T(8,128)S(1)} fusion(pred[16,911,158]{1,0,2:T(8,128)(4,1)S(1)} %get-tuple-element.497, f32[62,158]{1,0:T(8,128)S(1)} %broadcast_select_fusion.2, f32[62,158]{1,0:T(8,128)S(1)} %get-tuple-element.548, pred[62,158]{1,0:T(8,128)(4,1)S(1)} %broadcast_and_fusion.2, pred[16,158]{1,0:T(8,128)(4,1)S(1)} %get-tuple-element.498, ...), kind=kOutput, calls=%fused_computation.27.clone.1 | convolution fusion | flops 286356672 | bytes 3498240 | tf_op jit(solution)/shard_map/while/body/eval_jaxpr/cu,qut->qct/dot_general | solution.py:88
  175.0 4.1 %fusion.124 = f32[16,62,158]{2,1,0:T(8,128)S(1)} fusion(pred[16,911,158]{1,0,2:T(8,128)(4,1)S(1)} %get-tuple-element.494, f32[62,158]{1,0:T(8,128)S(1)} %broadcast_select_fusion.2, f32[62,158]{1,0:T(8,128)S(1)} %get-tuple-element.548, pred[16,158]{1,0:T(8,128)(4,1)S(1)} %get-tuple-element.496, pred[62,158]{1,0:T(8,128)(4,1)S(1)} %broadcast_and_fusion.2, ...), kind=kOutput, calls=%fused_computation.28.clone.1 | convolution fusion | flops 286356672 | bytes 3498240 | tf_op jit(solution)/shard_map/while/body/eval_jaxpr/cu,qut->qct/dot_general | solution.py:88
  179.2 1.8 fusion.126
  182.5 1.3 fusion.129
  183.9 4.8 %iota_compare_fusion.3 = (pred[16,911,158]{1,0,2:T(8,128)(4,1)S(1)}, pred[16,911,158]{1,0,2:T(8,128)(4,1)S(1)}) fusion(s32[16]{0:T(128)S(1)} %get-tuple-element.492, s32[16]{0:T(128)S(1)} %get-tuple-element.493), kind=kLoop, calls=%fused_computation.9.clone.1 | loop fusion | flops 9212032 | bytes 4606144 | tf_op jit(solution)/shard_map/while/body/eval_jaxpr/eq | solution.py:87
  189.0 4.1 %fusion.125 = f32[16,62,158]{2,1,0:T(8,128)S(1)} fusion(pred[16,911,158]{1,0,2:T(8,128)(4,1)S(1)} %get-tuple-element.497, f32[62,158]{1,0:T(8,128)S(1)} %broadcast_select_fusion.2, f32[62,158]{1,0:T(8,128)S(1)} %get-tuple-element.548, pred[62,158]{1,0:T(8,128)(4,1)S(1)} %broadcast_and_fusion.2, pred[16,158]{1,0:T(8,128)(4,1)S(1)} %get-tuple-element.498, ...), kind=kOutput, calls=%fused_computation.27.clone.1 | convolution fusion | flops 286356672 | bytes 3498240 | tf_op jit(solution)/shard_map/while/body/eval_jaxpr/cu,qut->qct/dot_general | solution.py:88
  193.1 4.1 %fusion.124 = f32[16,62,158]{2,1,0:T(8,128)S(1)} fusion(pred[16,911,158]{1,0,2:T(8,128)(4,1)S(1)} %get-tuple-element.494, f32[62,158]{1,0:T(8,128)S(1)} %broadcast_select_fusion.2, f32[62,158]{1,0:T(8,128)S(1)} %get-tuple-element.548, pred[16,158]{1,0:T(8,128)(4,1)S(1)} %get-tuple-element.496, pred[62,158]{1,0:T(8,128)(4,1)S(1)} %broadcast_and_fusion.2, ...), kind=kOutput, calls=%fused_computation.28.clone.1 | convolution fusion | flops 286356672 | bytes 3498240 | tf_op jit(solution)/shard_map/while/body/eval_jaxpr/cu,qut->qct/dot_general | solution.py:88
  197.3 1.8 fusion.126
  200.6 1.3 fusion.129
  202.0 3.4 %pmax.7 = f32[32,128]{1,0:T(8,128)S(1)} all-reduce(f32[32,128]{1,0:T(8,128)S(1)} %get-tuple-element.212), channel_id=1, replica_groups=mesh['groups'=2,'track'=4,'across'=2,'disp'=2] {'disp'}, use_global_device_ids=true, to_apply=%region_5.6 | all-reduce | flops 4096 | bytes 32768 | tf_op jit(solution)/shard_map/pmax | solution.py:142
  205.3 3.6 %all-reduce = (f32[32,128]{1,0:T(8,128)S(1)}, f32[32,128]{1,0:T(8,128)S(1)}) all-reduce(f32[32,128]{1,0:T(8,128)S(1)} %get-tuple-element.374, f32[32,128]{1,0:T(8,128)S(1)} %get-tuple-element.373), channel_id=1, replica_groups=mesh['groups'=2,'track'=4,'across'=2,'disp'=2] {'disp'}, use_global_device_ids=true, to_apply=%region_6.7 | all-reduce | flops 8192 | bytes 65536 | tf_op jit(solution)/shard_map/psum | solution.py:144
  (129 shorter events, 17.0 us)
Async XLA Ops:
  1.4 6.5 %collective-permute-start = (bf16[3,32,15]{2,1,0:T(8,128)(2,1)S(1)}, bf16[3,32,15]{2,1,0:T(8,128)(2,1)S(1)}, u32[]{:S(2)}, u32[]{:S(2)}) collective-permute-start(bf16[3,32,15]{2,1,0:T(8,128)(2,1)S(1)} %get-tuple-element.375), channel_id=1, source_target_pairs={{0,4},{4,8},{8,12},{1,5},{5,9},{9,13},{2,6},{6,10},{10,14},{3,7},{... | collective-permute-start | bytes 8648 | tf_op jit(solution)/shard_map/ppermute | solution.py:29
  6.4 5.7 %collective-permute-start.1 = (bf16[3,32,15]{2,1,0:T(8,128)(2,1)S(1)}, bf16[3,32,15]{2,1,0:T(8,128)(2,1)S(1)}, u32[]{:S(2)}, u32[]{:S(2)}) collective-permute-start(bf16[3,32,15]{2,1,0:T(8,128)(2,1)S(1)} %get-tuple-element.376), channel_id=1, source_target_pairs={{4,0},{8,4},{12,8},{5,1},{9,5},{13,9},{6,2},{10,6},{14,10},{7,3},{... | collective-permute-start | bytes 8648 | tf_op jit(solution)/shard_map/ppermute | solution.py:30
  13.0 5.4 %collective-permute-start.2 = (bf16[3,15,158]{2,1,0:T(8,128)(2,1)S(1)}, bf16[3,15,158]{2,1,0:T(8,128)(2,1)S(1)}, u32[]{:S(2)}, u32[]{:S(2)}) collective-permute-start(bf16[3,15,158]{2,1,0:T(8,128)(2,1)S(1)} %get-tuple-element.371), channel_id=1, source_target_pairs={{0,2},{1,3},{4,6},{5,7},{8,10},{9,11},{12,14},{13,15},{16,18},{17,... | collective-permute-start | bytes 42668 | tf_op jit(solution)/shard_map/ppermute | solution.py:29
  16.4 5.7 %collective-permute-start.3 = (bf16[3,15,158]{2,1,0:T(8,128)(2,1)S(1)}, bf16[3,15,158]{2,1,0:T(8,128)(2,1)S(1)}, u32[]{:S(2)}, u32[]{:S(2)}) collective-permute-start(bf16[3,15,158]{2,1,0:T(8,128)(2,1)S(1)} %get-tuple-element.372), channel_id=1, source_target_pairs={{2,0},{3,1},{6,4},{7,5},{10,8},{11,9},{14,12},{15,13},{18,16},{19,... | collective-permute-start | bytes 42668 | tf_op jit(solution)/shard_map/ppermute | solution.py:30
  23.0 5.1 %collective-permute-start.4 = (bf16[2,62,128]{2,1,0:T(8,128)(2,1)S(1)}, bf16[2,62,128]{2,1,0:T(8,128)(2,1)S(1)}, u32[]{:S(2)}, u32[]{:S(2)}) collective-permute-start(bf16[2,62,128]{2,1,0:T(8,128)(2,1)S(1)} %slice.88), channel_id=1, source_target_pairs={{0,4},{4,8},{8,12},{1,5},{5,9},{9,13},{2,6},{6,10},{10,14},{3,7},{... | collective-permute-start | bytes 95240 | tf_op jit(solution)/shard_map/ppermute | solution.py:19
  28.1 5.8 %collective-permute-start.5 = (bf16[2,62,128]{2,1,0:T(8,128)(2,1)S(1)}, bf16[2,62,128]{2,1,0:T(8,128)(2,1)S(1)}, u32[]{:S(2)}, u32[]{:S(2)}) collective-permute-start(bf16[2,62,128]{2,1,0:T(8,128)(2,1)S(1)} %collective-permute-done.4), channel_id=1, source_target_pairs={{0,4},{4,8},{8,12},{1,5},{5,9},{9,13},{2,6},{6,10},{10,14},{3,7},{... | collective-permute-start | bytes 95240 | tf_op jit(solution)/shard_map/ppermute | solution.py:19
  33.9 5.8 %collective-permute-start.6 = (bf16[2,62,128]{2,1,0:T(8,128)(2,1)S(1)}, bf16[2,62,128]{2,1,0:T(8,128)(2,1)S(1)}, u32[]{:S(2)}, u32[]{:S(2)}) collective-permute-start(bf16[2,62,128]{2,1,0:T(8,128)(2,1)S(1)} %collective-permute-done.5), channel_id=1, source_target_pairs={{0,4},{4,8},{8,12},{1,5},{5,9},{9,13},{2,6},{6,10},{10,14},{3,7},{... | collective-permute-start | bytes 95240 | tf_op jit(solution)/shard_map/ppermute | solution.py:19
  39.7 5.8 %collective-permute-start.7 = (bf16[2,62,128]{2,1,0:T(8,128)(2,1)S(1)}, bf16[2,62,128]{2,1,0:T(8,128)(2,1)S(1)}, u32[]{:S(2)}, u32[]{:S(2)}) collective-permute-start(bf16[2,62,128]{2,1,0:T(8,128)(2,1)S(1)} %collective-permute-done.6), channel_id=1, source_target_pairs={{0,4},{4,8},{8,12},{1,5},{5,9},{9,13},{2,6},{6,10},{10,14},{3,7},{... | collective-permute-start | bytes 95240 | tf_op jit(solution)/shard_map/ppermute | solution.py:19
  45.5 6.2 %collective-permute-start.8 = (bf16[2,62,128]{2,1,0:T(8,128)(2,1)S(1)}, bf16[2,62,128]{2,1,0:T(8,128)(2,1)S(1)}, u32[]{:S(2)}, u32[]{:S(2)}) collective-permute-start(bf16[2,62,128]{2,1,0:T(8,128)(2,1)S(1)} %collective-permute-done.7), channel_id=1, source_target_pairs={{0,4},{4,8},{8,12},{1,5},{5,9},{9,13},{2,6},{6,10},{10,14},{3,7},{... | collective-permute-start | bytes 95240 | tf_op jit(solution)/shard_map/ppermute | solution.py:19
  51.7 5.4 %collective-permute-start.9 = (bf16[2,62,128]{2,1,0:T(8,128)(2,1)S(1)}, bf16[2,62,128]{2,1,0:T(8,128)(2,1)S(1)}, u32[]{:S(2)}, u32[]{:S(2)}) collective-permute-start(bf16[2,62,128]{2,1,0:T(8,128)(2,1)S(1)} %collective-permute-done.8), channel_id=1, source_target_pairs={{0,4},{4,8},{8,12},{1,5},{5,9},{9,13},{2,6},{6,10},{10,14},{3,7},{... | collective-permute-start | bytes 95240 | tf_op jit(solution)/shard_map/ppermute | solution.py:19
where the time goes:
time: 210 us
  matrix products  86.7 us (41%)
  other arithmetic  55.9 us (27%)
  starting transfers between devices  35 us (17%)
  waiting for transfers between devices  15.4 us (7%)
  blocking collectives  6.94 us (3%)
  local copies, waits for them, and re-layouts  6.63 us (3%)
    dot_general x16, matrix products, frame_block(): jnp.einsum('cu,qut->qct', window[frame_index], selector, preferred_elemen...  66 us
    eq x8, other arithmetic, frame_block(): window_index == target_index + begin[:, None, None]  38.6 us
    ppermute x6, starting transfers between devices, shifted_2(): lax.ppermute(value, axis, [(source, source + steps) for source in range(l...  24.1 us
    dot_general x8, matrix products, aggregate(): jnp.einsum('qcu,ut->qct', terms, row_band, precision=highest_precision)  14.7 us
    reduce_max x8, other arithmetic, block_step(): new_top = jnp.maximum(highest_seen, jnp.max(hypothesis_likelihoods, axis=0))  10 us
    ppermute x2, starting transfers between devices, extended_2(): before = lax.ppermute(last, axis, up)  8.34 us
    ppermute x2, waiting for transfers between devices, extended_2(): after = lax.ppermute(leading, axis, down)  7.97 us
    ppermute x6, waiting for transfers between devices, shifted_2(): lax.ppermute(value, axis, [(source, source + steps) for source in range(l...  7.21 us
  transfers between devices with their start and end apart: 10, of which 8 were waited for; matrix products, arithmetic and copies ran while one was open for 1% of the time, Pallas kernels for 0%

commit v1 on v0

v1 whole, which is shorter than its diff:
```python
import functools

import jax
import jax.numpy as jnp
from jax import lax
from jax.experimental import pallas as pl
from jax.experimental.pallas import tpu as pltpu
from jax.sharding import PartitionSpec as P

MAXD = 320
RADIUS = 15
HALO = RADIUS + 1
CLIP = 2.0
SHARPNESS = 0.005
INTERVAL = 64.0
BIG = 1e30
GROUP = 4
BATCH = 4


def kernel(
    sizes, offs, mask, r_ref, s1_ref, s2_ref, disp_out, soft_out,
    rx, window, refs, weights, terms, box, scores, top, tx, mrx,
    send_sem, recv_sem, msend, mrecv,
):
    track, across, disp, cols, rows, planes = sizes
    ext = cols + 2 * HALO
    wide = 2 * ext
    span = rows + 2 * HALO
    deep = -(-(2 * (MAXD - 1) + RADIUS) // rows)
    deep0 = -(-(MAXD - 1 + RADIUS) // rows)
    back = min(deep, track - 1)
    ahead = back + 1
    r = lax.axis_index("track")
    c = lax.axis_index("across")
    d = lax.axis_index("disp")
    images = (s1_ref, s2_ref, r_ref)

    def present(dr, dc):
        return (r + dr >= 0) & (r + dr < track) & (c + dc >= 0) & (c + dc < across)

    barrier = pltpu.get_barrier_semaphore()
    for dr in range(-back, back + 1):
        for dc in (-1, 0, 1):
            if dr == 0 and dc == 0:
                continue

            @pl.when(present(dr, dc))
            def _():
                pl.semaphore_signal(barrier, inc=1, device_id={"track": r + dr, "across": c + dc})

    for i in range(1, disp):
        pl.semaphore_signal(barrier, inc=1, device_id={"disp": lax.rem(d + i, disp)})
    n_rows = jnp.minimum(r, back) + jnp.minimum(track - 1 - r, back) + 1
    n_cols = jnp.minimum(c, 1) + jnp.minimum(across - 1 - c, 1) + 1
    pl.semaphore_wait(barrier, n_rows * n_cols - 1 + disp - 1)

    def needed(slot):
        if slot == ahead:
            return (0, 1, 2)
        if slot <= 1:
            return (0, 1, 2)
        return (0, 1) if slot <= deep0 else (1,)

    def shift_of(slot):
        return -1 if slot == ahead else slot

    def copy(slot, image, dc):
        if dc == 0:
            src, lo, n = images[image], HALO, cols
        elif dc == 1:
            src, lo, n = images[image].at[pl.ds(cols - HALO, HALO)], 0, HALO
        else:
            src, lo, n = images[image].at[pl.ds(0, HALO)], HALO + cols, HALO
        return pltpu.make_async_remote_copy(
            src_ref=src,
            dst_ref=rx.at[slot, image, pl.ds(lo, n)],
            send_sem=send_sem.at[slot, image, dc + 1],
            recv_sem=recv_sem.at[slot, image, dc + 1],
            device_id={"track": r + shift_of(slot), "across": c + dc},
        )

    def each_copy(slot):
        for dc in (-1, 0, 1):
            if shift_of(slot) == 0 and dc == 0:
                continue
            yield dc, needed(slot)

    for slot in list(range(back, -1, -1)) + [ahead]:
        for dc, imgs in each_copy(slot):

            @pl.when(present(shift_of(slot), dc))
            def _():
                for image in imgs:
                    copy(slot, image, dc).start()

    for i in range(3):
        rx[0, i, HALO : HALO + cols, :] = images[i][...]
    for slot in range(back + 2):
        for lo, edge in ((0, c == 0), (HALO + cols, c == across - 1)):

            @pl.when(edge)
            def _():
                for i in range(3):
                    rx[slot, i, lo : lo + HALO, :] = jnp.zeros((HALO, rows), jnp.bfloat16)

    for j in range(1, deep + 1):

        @pl.when(r - j < 0)
        def _():
            window[(deep - j) * rows : (deep - j + 1) * rows, :] = jnp.full((rows, wide), BIG, jnp.float32)

    for slot in range(deep0 + 1, back + 1):
        rx[slot, 0] = jnp.zeros((ext, rows), jnp.bfloat16)

    @pl.when(r == 0)
    def _():
        refs[0:HALO, :] = jnp.zeros((HALO, wide), jnp.float32)

    @pl.when(r == track - 1)
    def _():
        refs[HALO + rows :, :] = jnp.zeros((HALO, wide), jnp.float32)
        window[(deep + 1) * rows :, :] = jnp.zeros((HALO, wide), jnp.float32)

    w0 = mask[0, 0, 0].astype(jnp.float32)
    w1 = mask[1, 0, 0].astype(jnp.float32)
    share = jnp.where(w0 + w1 > 1.5, 0.5, 1.0)
    w0, w1 = w0 * share, w1 * share
    lanes = GROUP * cols
    k_lane = lax.broadcasted_iota(jnp.int32, (wide, lanes), 0)
    n_lane = lax.broadcasted_iota(jnp.int32, (wide, lanes), 1)
    column = k_lane % ext - HALO
    gcol = column + c * cols
    near = (
        (jnp.abs(column - n_lane % cols) <= RADIUS) & (gcol >= 0) & (gcol < across * cols)
    )
    frame_weight = jnp.where(near, jnp.where(k_lane < ext, w0, w1), 0.0)
    for q in range(GROUP):
        part = jnp.where(n_lane // cols == q, frame_weight, 0.0).astype(jnp.bfloat16)
        for half in range(2):
            lo = (2 * q + half) * wide
            weights[lo : lo + wide, :] = part

    def arrive(slot):
        for dc, imgs in each_copy(slot):

            @pl.when(present(-shift_of(slot), -dc))
            def _():
                for image in imgs:
                    copy(slot, image, dc).wait_recv()

    def sources(slot):
        both = rx[slot, 0:2].reshape(wide, rows).astype(jnp.float32)
        return both.T

    def reference_rows(slot):
        one = rx[slot, 2].astype(jnp.float32)
        return jnp.concatenate([one, one], axis=0).T

    arrive(0)
    window[deep * rows : (deep + 1) * rows, :] = sources(0)
    refs[HALO : HALO + rows, :] = reference_rows(0)

    @pl.when(r < track - 1)
    def _():
        arrive(ahead)
        window[(deep + 1) * rows :, :] = sources(ahead)[0:HALO]
        refs[HALO + rows :, :] = reference_rows(ahead)[0:HALO]

    for j in range(1, back + 1):

        @pl.when(r - j >= 0)
        def _():
            arrive(j)
            window[(deep - j) * rows : (deep - j + 1) * rows, :] = sources(j)
            if j == 1:
                refs[0:HALO, :] = reference_rows(j)[rows - HALO :]

    first_frame = lax.broadcasted_iota(jnp.int32, (span, wide), 1) < ext
    begin = deep * rows - HALO

    def one_plane(index, m, q):
        o = offs[index]
        near_rows = window[pl.ds(begin - o, span), :]
        far_rows = window[pl.ds(begin - 2 * o, span), :]
        sampled = jnp.where(first_frame, near_rows, far_rows)
        term = jnp.minimum(jnp.abs(refs[...] - sampled), CLIP)
        high = term.astype(jnp.bfloat16)
        low = (term - high.astype(jnp.float32)).astype(jnp.bfloat16)
        terms[m * span : (m + 1) * span, 2 * q * wide : (2 * q + 1) * wide] = high
        terms[m * span : (m + 1) * span, (2 * q + 1) * wide : (2 * q + 2) * wide] = low

    t_pos = r * rows + lax.broadcasted_iota(jnp.int32, (rows, lanes), 0)
    a_pos = c * cols + lax.broadcasted_iota(jnp.int32, (rows, lanes), 1) % cols

    def window_count(position, length):
        return (
            jnp.minimum(position + RADIUS, length - 1) - jnp.maximum(position - RADIUS, 0) + 1
        ).astype(jnp.float32)

    count = window_count(t_pos, track * rows) * window_count(a_pos, across * cols)
    scale = -1.0 / (SHARPNESS * count)
    has_before = jnp.where(r > 0, 1.0, 0.0)
    has_after = jnp.where(r < track - 1, 1.0, 0.0)
    top[...] = jnp.full((rows, lanes), -jnp.inf, jnp.float32)

    def batch_step(b, carry):
        for m in range(BATCH):
            for q in range(GROUP):
                one_plane(b * (BATCH * GROUP) + m * GROUP + q, m, q)
        summed = jnp.dot(terms[...], weights[...], preferred_element_type=jnp.float32)
        for m in range(BATCH):
            y = summed[m * span : (m + 1) * span]
            y = jnp.concatenate(
                [y[:HALO] * has_before, y[HALO : HALO + rows], y[HALO + rows :] * has_after], axis=0
            )
            total = y
            for k, step in enumerate((1, 2, 4)):
                box[m, k, 0:span, :] = total
                total = total + box[m, k, step : step + span, :]
            total = total[: span - 8] + total[8:]
            total = total[:rows] + total[HALO : HALO + rows] - y[:rows]
            score = total * scale
            scores[b * BATCH + m] = score
            top[...] = jnp.maximum(top[...], score)
        return carry

    lax.fori_loop(0, planes // (BATCH * GROUP), batch_step, 0)

    def over_blocks(x, op):
        step = cols
        while step < lanes:
            x = op(x, pltpu.roll(x, step, 1))
            step *= 2
        return x

    peak = over_blocks(top[...], jnp.maximum)
    block_of = lax.broadcasted_iota(jnp.int32, (1, lanes), 1) // cols
    part = 32
    masses, moments = [], []
    for lo in range(0, rows, part):
        high = peak[lo : lo + part]

        def gather(g, carry):
            mass, moment = carry
            value = jnp.zeros((1, lanes), jnp.float32)
            for q in range(GROUP):
                value = jnp.where(block_of == q, offs[g * GROUP + q].astype(jnp.float32), value)
            lifted = jnp.exp(scores[g, lo : lo + part, :] - high)
            return mass + lifted, moment + lifted * value

        zero = jnp.zeros((part, lanes), jnp.float32)
        mass, moment = lax.fori_loop(0, planes // GROUP, gather, (zero, zero), unroll=4)
        masses.append(mass)
        moments.append(moment)
    mass = over_blocks(jnp.concatenate(masses, axis=0), jnp.add)
    moment = over_blocks(jnp.concatenate(moments, axis=0), jnp.add)
    own = [x.T[0:cols] for x in (peak, mass, moment)]
    for k in range(3):
        tx[k] = own[k]

    def merge_copy(i):
        return pltpu.make_async_remote_copy(
            src_ref=tx,
            dst_ref=mrx.at[i - 1],
            send_sem=msend.at[i - 1],
            recv_sem=mrecv.at[i - 1],
            device_id={"disp": lax.rem(d + i, disp)},
        )

    for i in range(1, disp):
        merge_copy(i).start()
    for slot in range(back + 2):
        for dc, imgs in each_copy(slot):

            @pl.when(present(shift_of(slot), dc))
            def _():
                for image in imgs:
                    copy(slot, image, dc).wait_send()

    peak, mass, moment = own
    for i in range(1, disp):
        merge_copy(i).wait_recv()
        other = [mrx[i - 1, k] for k in range(3)]
        new = jnp.maximum(peak, other[0])
        mine, theirs = jnp.exp(peak - new), jnp.exp(other[0] - new)
        mass = mass * mine + other[1] * theirs
        moment = moment * mine + other[2] * theirs
        peak = new
    disp_out[...] = moment / mass / INTERVAL
    soft_out[...] = -SHARPNESS * (peak + jnp.log(mass))
    for i in range(1, disp):
        merge_copy(i).wait_send()


def shards(track, across, disp, ref_image, source_one, source_two, plane_offsets, intersection_mask):
    cols, rows = ref_image.shape
    planes = plane_offsets.shape[0]
    ext = cols + 2 * HALO
    wide, span, lanes = 2 * ext, rows + 2 * HALO, GROUP * cols
    deep = -(-(2 * (MAXD - 1) + RADIUS) // rows)
    back = min(deep, track - 1)
    vmem = pl.BlockSpec(memory_space=pltpu.VMEM)
    smem = pl.BlockSpec(memory_space=pltpu.SMEM)
    out = jax.ShapeDtypeStruct((cols, rows), jnp.float32)
    return pl.pallas_call(
        functools.partial(kernel, (track, across, disp, cols, rows, planes)),
        out_shape=(out, out),
        in_specs=[smem, smem, vmem, vmem, vmem],
        out_specs=(vmem, vmem),
        scratch_shapes=[
            pltpu.VMEM((back + 2, 3, ext, rows), jnp.bfloat16),
            pltpu.VMEM(((deep + 1) * rows + HALO, wide), jnp.float32),
            pltpu.VMEM((span, wide), jnp.float32),
            pltpu.VMEM((2 * GROUP * wide, lanes), jnp.bfloat16),
            pltpu.VMEM((BATCH * span, 2 * GROUP * wide), jnp.bfloat16),
            pltpu.VMEM((BATCH, 3, span + 8, lanes), jnp.float32),
            pltpu.VMEM((planes // GROUP, rows, lanes), jnp.float32),
            pltpu.VMEM((rows, lanes), jnp.float32),
            pltpu.VMEM((3, cols, rows), jnp.float32),
            pltpu.VMEM((max(disp - 1, 1), 3, cols, rows), jnp.float32),
            pltpu.SemaphoreType.DMA((back + 2, 3, 3)),
            pltpu.SemaphoreType.DMA((back + 2, 3, 3)),
            pltpu.SemaphoreType.DMA((max(disp - 1, 1),)),
            pltpu.SemaphoreType.DMA((max(disp - 1, 1),)),
        ],
        compiler_params=pltpu.CompilerParams(collective_id=0, has_side_effects=True),
    )(plane_offsets, intersection_mask, ref_image, source_one, source_two)


def solution(mesh):
    sizes = (mesh.shape["track"], mesh.shape["across"], mesh.shape["disp"])
    tiles = P(("groups", "across"), "track")
    return jax.shard_map(
        functools.partial(shards, *sizes),
        mesh=mesh,
        in_specs=(tiles, tiles, tiles, P("disp"), P(None, ("groups", "across"), "track")),
        out_specs=(tiles, tiles),
        check_vma=False,
    )
```

time: 210 us -> 23.9 us (0.11)
  matrix products: 86.7 us -> 0 us
  other arithmetic: 55.9 us -> 0 us
  starting transfers between devices: 35 us -> 0 us
  Pallas kernels: 0 us -> 19.8 us
  waiting for transfers between devices: 15.4 us -> 0 us
  blocking collectives: 6.94 us -> 0 us
  local copies, waits for them, and re-layouts: 6.63 us -> 3.24 us
    dot_general x32 -> x0, matrix products: 86.7 us -> none  [the longest x16 66 us: frame_block(): jnp.einsum('cu,qut->qct', window[frame_index], selector, preferred_elemen...]
    eq x8 -> x0, other arithmetic: 38.6 us -> none  [frame_block(): window_index == target_index + begin[:, None, None]]
    ppermute x10 -> x0, starting transfers between devices: 35 us -> none  [the longest x6 24.1 us: shifted_2(): lax.ppermute(value, axis, [(source, source + steps) for source in range(l...]
    pallas_call x0 -> x1, Pallas kernels: none -> 19.8 us  [shards(): pl.pallas_call(functools.partial(kernel, (track, across, disp, cols, rows...]
    ppermute x10 -> x0, waiting for transfers between devices: 15.4 us -> none  [the longest x2 7.97 us: extended_2(): after = lax.ppermute(leading, axis, down)]
    reduce_max x8 -> x0, other arithmetic: 10 us -> none  [block_step(): new_top = jnp.maximum(highest_seen, jnp.max(hypothesis_likelihoods, axis=0))]
    slice x12 -> x0, local copies, waits for them, and re-layouts: 5.71 us -> none  [the longest x8 4.93 us: block_step(): masks[0] * means[:block] + masks[1] * means[block:]]
    psum x1 -> x0, blocking collectives: 3.58 us -> none  [shards(): lax.psum((normalizer_mass * fading, disparity_moment_accumulator * fading...]
  transfers between devices with their start and end apart: 10 -> 0, of which waited for: 8 -> 0; matrix products, arithmetic and copies ran while one was open for 1% -> 0% of each run, Pallas kernels for 0% -> 0%
where the time goes in v1:
time: 23.9 us; the launch traced here: 23.7 us
  Pallas kernels  19.8 us (83%)
  local copies, waits for them, and re-layouts  3.24 us (14%)
  between operations  0.65 us (3%)
    pallas_call x1, Pallas kernels, shards(): pl.pallas_call(functools.partial(kernel, (track, across, disp, cols, rows...  19.8 us
    unnamed x5, local copies, waits for them, and re-layouts  3.24 us

profile of v1, /device:TPU:0, one launch (start us, length us, event | category | flops | bytes accessed | tf_op | source)
XLA Modules:
  0.0 23.7 jit_solution(12766683759308347454)
XLA Ops:
  0.6 1.3 %copy.7.mask = s32[2,1,1]{2,1,0:T(1,128)} copy(s32[2,1,1]{0,2,1:T(1,128)} %param.9) | data formatting | bytes 16 | tf_op args[4]
  1.9 19.8 %shard_map.68 = (f32[32,128]{1,0:T(8,128)}, f32[32,128]{1,0:T(8,128)}) custom-call(s32[128]{0:T(128)} %offs.1, s32[2,1,1]{2,1,0:T(1,128)} %copy.7.mask, bf16[32,128]{1,0:T(8,128)(2,1)} %r_ref.1, bf16[32,128]{1,0:T(8,128)(2,1)} %s1_ref.1, bf16[32,128]{1,0:T(8,128)(2,1)} %s2_ref.1), custom_call_target="tpu_custom_call" | custom-call | tf_op jit(solution)/shard_map/pallas_call | solution.py:306
  21.8 0.0 copy-start
  21.8 1.3 %copy.10 = f32[32,128]{1,0:T(8,128)} copy(f32[32,128]{1,0:T(8,128)} %get-tuple-element.4) | data formatting | bytes 32768
  23.1 0.0 copy-done
  23.1 0.6 %copy.11 = f32[32,128]{1,0:T(8,128)} copy(f32[32,128]{1,0:T(8,128)S(1)} %copy-done) | data formatting | bytes 32768
Async XLA Ops:
  21.8 1.3 %copy-start = (f32[32,128]{1,0:T(8,128)S(1)}, f32[32,128]{1,0:T(8,128)}, u32[]{:S(2)}) copy-start(f32[32,128]{1,0:T(8,128)} %get-tuple-element.5) | copy-start | bytes 49156

commit v2 on v1

--- a/solution.py
+++ b/solution.py
@@ -19,9 +19,9 @@
 
 
 def kernel(
-    sizes, offs, mask, r_ref, s1_ref, s2_ref, disp_out, soft_out,
-    rx, window, refs, weights, terms, box, scores, top, tx, mrx,
-    send_sem, recv_sem, msend, mrecv,
+    sizes, offs_hbm, mask_hbm, r_ref, s1_ref, s2_ref, out,
+    offs, mask, rx, window0, window1, refs0, refs1, weights, terms_even, terms_odd, box, scores, scales, top, tx, mrx,
+    send_sem, recv_sem, msend, mrecv, local_sem,
 ):
     track, across, disp, cols, rows, planes = sizes
     ext = cols + 2 * HALO
@@ -51,10 +51,16 @@
 
     for i in range(1, disp):
         pl.semaphore_signal(barrier, inc=1, device_id={"disp": lax.rem(d + i, disp)})
+    local = [
+        pltpu.make_async_copy(offs_hbm, offs, local_sem.at[3]),
+        pltpu.make_async_copy(mask_hbm, mask, local_sem.at[4]),
+    ] + [
+        pltpu.make_async_copy(images[i], rx.at[0, i, pl.ds(HALO, cols)], local_sem.at[i]) for i in range(3)
+    ]
+    for one in local:
+        one.start()
     n_rows = jnp.minimum(r, back) + jnp.minimum(track - 1 - r, back) + 1
     n_cols = jnp.minimum(c, 1) + jnp.minimum(across - 1 - c, 1) + 1
-    pl.semaphore_wait(barrier, n_rows * n_cols - 1 + disp - 1)
-
     def needed(slot):
         if slot == ahead:
             return (0, 1, 2)
@@ -86,16 +92,6 @@
                 continue
             yield dc, needed(slot)
 
-    for slot in list(range(back, -1, -1)) + [ahead]:
-        for dc, imgs in each_copy(slot):
-
-            @pl.when(present(shift_of(slot), dc))
-            def _():
-                for image in imgs:
-                    copy(slot, image, dc).start()
-
-    for i in range(3):
-        rx[0, i, HALO : HALO + cols, :] = images[i][...]
     for slot in range(back + 2):
         for lo, edge in ((0, c == 0), (HALO + cols, c == across - 1)):
 
@@ -108,24 +104,23 @@
 
         @pl.when(r - j < 0)
         def _():
-            window[(deep - j) * rows : (deep - j + 1) * rows, :] = jnp.full((rows, wide), BIG, jnp.float32)
+            for window in (window0, window1):
+                window[(deep - j) * rows : (deep - j + 1) * rows, :] = jnp.full((rows, wide), BIG, jnp.float32)
 
     for slot in range(deep0 + 1, back + 1):
         rx[slot, 0] = jnp.zeros((ext, rows), jnp.bfloat16)
 
     @pl.when(r == 0)
     def _():
-        refs[0:HALO, :] = jnp.zeros((HALO, wide), jnp.float32)
+        for refs in (refs0, refs1):
+            refs[0:HALO, :] = jnp.zeros((HALO, wide), jnp.float32)
 
     @pl.when(r == track - 1)
     def _():
-        refs[HALO + rows :, :] = jnp.zeros((HALO, wide), jnp.float32)
-        window[(deep + 1) * rows :, :] = jnp.zeros((HALO, wide), jnp.float32)
-
-    w0 = mask[0, 0, 0].astype(jnp.float32)
-    w1 = mask[1, 0, 0].astype(jnp.float32)
-    share = jnp.where(w0 + w1 > 1.5, 0.5, 1.0)
-    w0, w1 = w0 * share, w1 * share
+        for refs, window in ((refs0, window0), (refs1, window1)):
+            refs[HALO + rows :, :] = jnp.zeros((HALO, wide), jnp.float32)
+            window[(deep + 1) * rows :, :] = jnp.zeros((HALO, wide), jnp.float32)
+
     lanes = GROUP * cols
     k_lane = lax.broadcasted_iota(jnp.int32, (wide, lanes), 0)
     n_lane = lax.broadcasted_iota(jnp.int32, (wide, lanes), 1)
@@ -134,61 +129,12 @@
     near = (
         (jnp.abs(column - n_lane % cols) <= RADIUS) & (gcol >= 0) & (gcol < across * cols)
     )
-    frame_weight = jnp.where(near, jnp.where(k_lane < ext, w0, w1), 0.0)
-    for q in range(GROUP):
-        part = jnp.where(n_lane // cols == q, frame_weight, 0.0).astype(jnp.bfloat16)
+    for p in range(GROUP // 2):
+        hit = near & (n_lane // cols == 2 * p + k_lane // ext)
+        part = jnp.where(hit, 1.0, 0.0).astype(jnp.bfloat16)
         for half in range(2):
-            lo = (2 * q + half) * wide
+            lo = (2 * p + half) * wide
             weights[lo : lo + wide, :] = part
-
-    def arrive(slot):
-        for dc, imgs in each_copy(slot):
-
-            @pl.when(present(-shift_of(slot), -dc))
-            def _():
-                for image in imgs:
-                    copy(slot, image, dc).wait_recv()
-
-    def sources(slot):
-        both = rx[slot, 0:2].reshape(wide, rows).astype(jnp.float32)
-        return both.T
-
-    def reference_rows(slot):
-        one = rx[slot, 2].astype(jnp.float32)
-        return jnp.concatenate([one, one], axis=0).T
-
-    arrive(0)
-    window[deep * rows : (deep + 1) * rows, :] = sources(0)
-    refs[HALO : HALO + rows, :] = reference_rows(0)
-
-    @pl.when(r < track - 1)
-    def _():
-        arrive(ahead)
-        window[(deep + 1) * rows :, :] = sources(ahead)[0:HALO]
-        refs[HALO + rows :, :] = reference_rows(ahead)[0:HALO]
-
-    for j in range(1, back + 1):
-
-        @pl.when(r - j >= 0)
-        def _():
-            arrive(j)
-            window[(deep - j) * rows : (deep - j + 1) * rows, :] = sources(j)
-            if j == 1:
-                refs[0:HALO, :] = reference_rows(j)[rows - HALO :]
-
-    first_frame = lax.broadcasted_iota(jnp.int32, (span, wide), 1) < ext
-    begin = deep * rows - HALO
-
-    def one_plane(index, m, q):
-        o = offs[index]
-        near_rows = window[pl.ds(begin - o, span), :]
-        far_rows = window[pl.ds(begin - 2 * o, span), :]
-        sampled = jnp.where(first_frame, near_rows, far_rows)
-        term = jnp.minimum(jnp.abs(refs[...] - sampled), CLIP)
-        high = term.astype(jnp.bfloat16)
-        low = (term - high.astype(jnp.float32)).astype(jnp.bfloat16)
-        terms[m * span : (m + 1) * span, 2 * q * wide : (2 * q + 1) * wide] = high
-        terms[m * span : (m + 1) * span, (2 * q + 1) * wide : (2 * q + 2) * wide] = low
 
     t_pos = r * rows + lax.broadcasted_iota(jnp.int32, (rows, lanes), 0)
     a_pos = c * cols + lax.broadcasted_iota(jnp.int32, (rows, lanes), 1) % cols
@@ -199,16 +145,97 @@
         ).astype(jnp.float32)
 
     count = window_count(t_pos, track * rows) * window_count(a_pos, across * cols)
-    scale = -1.0 / (SHARPNESS * count)
+    scales[...] = -1.0 / (SHARPNESS * count)
     has_before = jnp.where(r > 0, 1.0, 0.0)
     has_after = jnp.where(r < track - 1, 1.0, 0.0)
     top[...] = jnp.full((rows, lanes), -jnp.inf, jnp.float32)
 
-    def batch_step(b, carry):
+    pl.semaphore_wait(barrier, n_rows * n_cols - 1 + disp - 1)
+
+    for slot in list(range(back, -1, -1)) + [ahead]:
+        for dc, imgs in each_copy(slot):
+
+            @pl.when(present(shift_of(slot), dc))
+            def _():
+                for image in imgs:
+                    copy(slot, image, dc).start()
+
+    for one in local:
+        one.wait()
+    w0 = mask[0, 0, 0].astype(jnp.float32)
+    w1 = mask[0, 0, 1].astype(jnp.float32)
+    share = jnp.where(w0 + w1 > 1.5, 0.5, 1.0)
+    w0, w1 = w0 * share, w1 * share
+
+    def arrive(slot):
+        for dc, imgs in each_copy(slot):
+
+            @pl.when(present(-shift_of(slot), -dc))
+            def _():
+                for image in imgs:
+                    copy(slot, image, dc).wait_recv()
+
+    first_half = lax.broadcasted_iota(jnp.int32, (1, wide), 1) < ext
+
+    def place_sources(slot, lo, n):
+        both = rx[slot, 0:2].reshape(wide, rows).astype(jnp.float32).T[0:n]
+        swapped = pltpu.roll(both, ext, 1)
+        window0[lo : lo + n, :] = jnp.where(first_half, both, swapped) * w0
+        window1[lo : lo + n, :] = jnp.where(first_half, swapped, both) * w1
+
+    def place_reference(slot, lo, start, n):
+        one = rx[slot, 2].astype(jnp.float32)
+        both = jnp.concatenate([one, one], axis=0).T[start : start + n]
+        refs0[lo : lo + n, :] = both * w0
+        refs1[lo : lo + n, :] = both * w1
+
+    arrive(0)
+    place_sources(0, deep * rows, rows)
+    place_reference(0, HALO, 0, rows)
+
+    @pl.when(r < track - 1)
+    def _():
+        arrive(ahead)
+        place_sources(ahead, (deep + 1) * rows, HALO)
+        place_reference(ahead, HALO + rows, 0, HALO)
+
+    for j in range(1, back + 1):
+
+        @pl.when(r - j >= 0)
+        def _():
+            arrive(j)
+            place_sources(j, (deep - j) * rows, rows)
+            if j == 1:
+                place_reference(j, 0, rows - HALO, HALO)
+
+    first = lax.broadcasted_iota(jnp.int32, (span, wide), 1) < ext
+    begin = deep * rows - HALO
+    clip0, clip1 = CLIP * w0, CLIP * w1
+
+    def one_pair(index, terms, m, p):
+        o, q = offs[index], offs[index + 1]
+
+        def part(window, refs, clip, times):
+            sampled = jnp.where(
+                first, window[pl.ds(begin - times * o, span), :], window[pl.ds(begin - times * q, span), :]
+            )
+            return jnp.minimum(jnp.abs(refs[...] - sampled), clip)
+
+        term = part(window0, refs0, clip0, 1) + part(window1, refs1, clip1, 2)
+        high = term.astype(jnp.bfloat16)
+        low = (term - high.astype(jnp.float32)).astype(jnp.bfloat16)
+        terms[m * span : (m + 1) * span, 2 * p * wide : (2 * p + 1) * wide] = high
+        terms[m * span : (m + 1) * span, (2 * p + 1) * wide : (2 * p + 2) * wide] = low
+
+    def fill(b, terms):
         for m in range(BATCH):
-            for q in range(GROUP):
-                one_plane(b * (BATCH * GROUP) + m * GROUP + q, m, q)
-        summed = jnp.dot(terms[...], weights[...], preferred_element_type=jnp.float32)
+            for p in range(GROUP // 2):
+                one_pair(b * (BATCH * GROUP) + m * GROUP + 2 * p, terms, m, p)
+
+    def multiply(terms):
+        return jnp.dot(terms[...], weights[...], preferred_element_type=jnp.float32)
+
+    def finish(b, summed):
         for m in range(BATCH):
             y = summed[m * span : (m + 1) * span]
             y = jnp.concatenate(
@@ -220,12 +247,27 @@
                 total = total + box[m, k, step : step + span, :]
             total = total[: span - 8] + total[8:]
             total = total[:rows] + total[HALO : HALO + rows] - y[:rows]
-            score = total * scale
+            score = total * scales[...]
             scores[b * BATCH + m] = score
             top[...] = jnp.maximum(top[...], score)
+
+    batches = planes // (BATCH * GROUP)
+
+    def two_batches(i, carry):
+        summed = multiply(terms_even)
+        fill(2 * i + 1, terms_odd)
+        finish(2 * i, summed)
+        summed = multiply(terms_odd)
+        fill(2 * i + 2, terms_even)
+        finish(2 * i + 1, summed)
         return carry
 
-    lax.fori_loop(0, planes // (BATCH * GROUP), batch_step, 0)
+    fill(0, terms_even)
+    lax.fori_loop(0, batches // 2 - 1, two_batches, 0)
+    summed = multiply(terms_even)
+    fill(batches - 1, terms_odd)
+    finish(batches - 2, summed)
+    finish(batches - 1, multiply(terms_odd))
 
     def over_blocks(x, op):
         step = cols
@@ -287,8 +329,7 @@
         mass = mass * mine + other[1] * theirs
         moment = moment * mine + other[2] * theirs
         peak = new
-    disp_out[...] = moment / mass / INTERVAL
-    soft_out[...] = -SHARPNESS * (peak + jnp.log(mass))
+    out[0], out[1], out[2] = peak, mass, moment
     for i in range(1, disp):
         merge_copy(i).wait_send()
 
@@ -301,31 +342,43 @@
     deep = -(-(2 * (MAXD - 1) + RADIUS) // rows)
     back = min(deep, track - 1)
     vmem = pl.BlockSpec(memory_space=pltpu.VMEM)
-    smem = pl.BlockSpec(memory_space=pltpu.SMEM)
-    out = jax.ShapeDtypeStruct((cols, rows), jnp.float32)
-    return pl.pallas_call(
+    anywhere = pl.BlockSpec(memory_space=pl.ANY)
+    f32 = jnp.float32
+    window = pltpu.VMEM(((deep + 1) * rows + HALO, wide), f32)
+    refs = pltpu.VMEM((span, wide), f32)
+    terms = pltpu.VMEM((BATCH * span, GROUP * wide), jnp.bfloat16)
+    merged = pl.pallas_call(
         functools.partial(kernel, (track, across, disp, cols, rows, planes)),
-        out_shape=(out, out),
-        in_specs=[smem, smem, vmem, vmem, vmem],
-        out_specs=(vmem, vmem),
+        out_shape=jax.ShapeDtypeStruct((3, cols, rows), f32),
+        in_specs=[anywhere] * 5,
+        out_specs=vmem,
         scratch_shapes=[
+            pltpu.SMEM((planes,), jnp.int32),
+            pltpu.SMEM((1, 1, 2), jnp.int32),
             pltpu.VMEM((back + 2, 3, ext, rows), jnp.bfloat16),
-            pltpu.VMEM(((deep + 1) * rows + HALO, wide), jnp.float32),
-            pltpu.VMEM((span, wide), jnp.float32),
-            pltpu.VMEM((2 * GROUP * wide, lanes), jnp.bfloat16),
-            pltpu.VMEM((BATCH * span, 2 * GROUP * wide), jnp.bfloat16),
-            pltpu.VMEM((BATCH, 3, span + 8, lanes), jnp.float32),
-            pltpu.VMEM((planes // GROUP, rows, lanes), jnp.float32),
-            pltpu.VMEM((rows, lanes), jnp.float32),
-            pltpu.VMEM((3, cols, rows), jnp.float32),
-            pltpu.VMEM((max(disp - 1, 1), 3, cols, rows), jnp.float32),
+            window,
+            window,
+            refs,
+            refs,
+            pltpu.VMEM((GROUP * wide, lanes), jnp.bfloat16),
+            terms,
+            terms,
+            pltpu.VMEM((BATCH, 3, span + 8, lanes), f32),
+            pltpu.VMEM((planes // GROUP, rows, lanes), f32),
+            pltpu.VMEM((rows, lanes), f32),
+            pltpu.VMEM((rows, lanes), f32),
+            pltpu.VMEM((3, cols, rows), f32),
+            pltpu.VMEM((max(disp - 1, 1), 3, cols, rows), f32),
             pltpu.SemaphoreType.DMA((back + 2, 3, 3)),
             pltpu.SemaphoreType.DMA((back + 2, 3, 3)),
             pltpu.SemaphoreType.DMA((max(disp - 1, 1),)),
             pltpu.SemaphoreType.DMA((max(disp - 1, 1),)),
+            pltpu.SemaphoreType.DMA((5,)),
         ],
         compiler_params=pltpu.CompilerParams(collective_id=0, has_side_effects=True),
-    )(plane_offsets, intersection_mask, ref_image, source_one, source_two)
+    )(plane_offsets, jnp.transpose(intersection_mask, (1, 2, 0)), ref_image, source_one, source_two)
+    peak, mass, moment = merged[0], merged[1], merged[2]
+    return moment / mass / INTERVAL, -SHARPNESS * (peak + jnp.log(mass))
 
 
 def solution(mesh):

time: 23.9 us -> 19.8 us (0.83)
  local copies, waits for them, and re-layouts: 3.24 us -> 0 us
  Pallas kernels: 19.8 us -> 17.6 us
  other arithmetic: 0 us -> 1.38 us
    unnamed x5 -> x0, local copies, waits for them, and re-layouts: 3.24 us -> none
    pallas_call x1, Pallas kernels: 19.8 us -> 17.6 us  [shards(): pl.pallas_call(functools.partial(kernel, (track, across, disp, cols, rows...]
    mul x0 -> x1, other arithmetic: none -> 1.38 us  [shards(): return (moment / mass / INTERVAL, -SHARPNESS * (peak + jnp.log(mass)))]
where the time goes in v2:
time: 19.8 us; the launch traced here: 19.6 us
  Pallas kernels  17.6 us (89%)
  other arithmetic  1.38 us (7%)
  between operations  0.64 us (3%)
    pallas_call x1, Pallas kernels, shards(): pl.pallas_call(functools.partial(kernel, (track, across, disp, cols, rows...  17.6 us
    mul x1, other arithmetic, shards(): return (moment / mass / INTERVAL, -SHARPNESS * (peak + jnp.log(mass)))  1.38 us

profile of v2, /device:TPU:0, one launch (start us, length us, event | category | flops | bytes accessed | tf_op | source)
XLA Modules:
  0.0 19.6 jit_solution(2190928681070860081)
XLA Ops:
  0.6 17.6 %shard_map.68 = f32[3,32,128]{2,1,0:T(8,128)} custom-call(s32[128]{0:T(128)} %offs_hbm.1, s32[1,1,2]{2,1,0:T(1,128)} %bitcast.5, bf16[32,128]{1,0:T(8,128)(2,1)} %r_ref.1, bf16[32,128]{1,0:T(8,128)(2,1)} %s1_ref.1, bf16[32,128]{1,0:T(8,128)(2,1)} %s2_ref.1), custom_call_target="tpu_custom_call" | custom-call | tf_op jit(solution)/shard_map/pallas_call | solution.py:350
  18.2 1.4 %multiply_bitcast_fusion = (f32[32,128]{1,0:T(8,128)}, f32[32,128]{1,0:T(8,128)}) fusion(f32[3,32,128]{2,1,0:T(8,128)} %shard_map.68), kind=kLoop, calls=%fused_computation | loop fusion | flops 16384 | bytes 81920 | tf_op jit(solution)/shard_map/mul | solution.py:381

commit v3 on v2

--- a/solution.py
+++ b/solution.py
@@ -15,6 +15,9 @@
 INTERVAL = 64.0
 BIG = 1e30
 GROUP = 4
+ROUNDER = 1.5 * 2.0**16
+LOG2E = 1.4426950408889634
+LN2 = 0.6931471805599453
 BATCH = 4
 
 
@@ -36,21 +39,27 @@
     d = lax.axis_index("disp")
     images = (s1_ref, s2_ref, r_ref)
 
+    def at(dr, dc):
+        return {"track": r + dr, "across": c + dc}
+
+    def beside(i):
+        return {"disp": lax.rem(d + i, disp)}
+
     def present(dr, dc):
         return (r + dr >= 0) & (r + dr < track) & (c + dc >= 0) & (c + dc < across)
 
     barrier = pltpu.get_barrier_semaphore()
-    for dr in range(-back, back + 1):
+    for dr in sorted(range(-back, back + 1), key=abs, reverse=True):
         for dc in (-1, 0, 1):
             if dr == 0 and dc == 0:
                 continue
 
             @pl.when(present(dr, dc))
             def _():
-                pl.semaphore_signal(barrier, inc=1, device_id={"track": r + dr, "across": c + dc})
+                pl.semaphore_signal(barrier, inc=1, device_id=at(dr, dc))
 
     for i in range(1, disp):
-        pl.semaphore_signal(barrier, inc=1, device_id={"disp": lax.rem(d + i, disp)})
+        pl.semaphore_signal(barrier, inc=1, device_id=beside(i))
     local = [
         pltpu.make_async_copy(offs_hbm, offs, local_sem.at[3]),
         pltpu.make_async_copy(mask_hbm, mask, local_sem.at[4]),
@@ -61,36 +70,25 @@
         one.start()
     n_rows = jnp.minimum(r, back) + jnp.minimum(track - 1 - r, back) + 1
     n_cols = jnp.minimum(c, 1) + jnp.minimum(across - 1 - c, 1) + 1
-    def needed(slot):
-        if slot == ahead:
-            return (0, 1, 2)
-        if slot <= 1:
-            return (0, 1, 2)
-        return (0, 1) if slot <= deep0 else (1,)
-
     def shift_of(slot):
         return -1 if slot == ahead else slot
 
-    def copy(slot, image, dc):
-        if dc == 0:
-            src, lo, n = images[image], HALO, cols
-        elif dc == 1:
-            src, lo, n = images[image].at[pl.ds(cols - HALO, HALO)], 0, HALO
+    def copy(slot, dc):
+        if slot <= 1 or slot == ahead:
+            some = pl.ds(0, 3)
         else:
-            src, lo, n = images[image].at[pl.ds(0, HALO)], HALO + cols, HALO
+            some = pl.ds(0, 2) if slot <= deep0 else pl.ds(1, 1)
+        start, lo, n = {0: (0, HALO, cols), 1: (cols - HALO, 0, HALO), -1: (0, HALO + cols, HALO)}[dc]
         return pltpu.make_async_remote_copy(
-            src_ref=src,
-            dst_ref=rx.at[slot, image, pl.ds(lo, n)],
-            send_sem=send_sem.at[slot, image, dc + 1],
-            recv_sem=recv_sem.at[slot, image, dc + 1],
-            device_id={"track": r + shift_of(slot), "across": c + dc},
+            src_ref=rx.at[0, some, pl.ds(HALO + start, n)],
+            dst_ref=rx.at[slot, some, pl.ds(lo, n)],
+            send_sem=send_sem.at[slot, dc + 1],
+            recv_sem=recv_sem.at[slot, dc + 1],
+            device_id=at(shift_of(slot), dc),
         )
 
-    def each_copy(slot):
-        for dc in (-1, 0, 1):
-            if shift_of(slot) == 0 and dc == 0:
-                continue
-            yield dc, needed(slot)
+    def sides(slot):
+        return (-1, 1) if slot == 0 else (-1, 0, 1)
 
     for slot in range(back + 2):
         for lo, edge in ((0, c == 0), (HALO + cols, c == across - 1)):
@@ -145,35 +143,33 @@
         ).astype(jnp.float32)
 
     count = window_count(t_pos, track * rows) * window_count(a_pos, across * cols)
-    scales[...] = -1.0 / (SHARPNESS * count)
+    scales[...] = -LOG2E / (SHARPNESS * count)
     has_before = jnp.where(r > 0, 1.0, 0.0)
     has_after = jnp.where(r < track - 1, 1.0, 0.0)
     top[...] = jnp.full((rows, lanes), -jnp.inf, jnp.float32)
 
-    pl.semaphore_wait(barrier, n_rows * n_cols - 1 + disp - 1)
-
-    for slot in list(range(back, -1, -1)) + [ahead]:
-        for dc, imgs in each_copy(slot):
-
-            @pl.when(present(shift_of(slot), dc))
-            def _():
-                for image in imgs:
-                    copy(slot, image, dc).start()
-
     for one in local:
         one.wait()
+    pl.semaphore_wait(barrier, n_rows * n_cols - 1 + disp - 1)
+
+    for slot in list(range(back, -1, -1)) + [ahead]:
+        for dc in sides(slot):
+
+            @pl.when(present(shift_of(slot), dc))
+            def _():
+                copy(slot, dc).start()
+
     w0 = mask[0, 0, 0].astype(jnp.float32)
     w1 = mask[0, 0, 1].astype(jnp.float32)
     share = jnp.where(w0 + w1 > 1.5, 0.5, 1.0)
     w0, w1 = w0 * share, w1 * share
 
     def arrive(slot):
-        for dc, imgs in each_copy(slot):
+        for dc in sides(slot):
 
             @pl.when(present(-shift_of(slot), -dc))
             def _():
-                for image in imgs:
-                    copy(slot, image, dc).wait_recv()
+                copy(slot, dc).wait_recv()
 
     first_half = lax.broadcasted_iota(jnp.int32, (1, wide), 1) < ext
 
@@ -222,10 +218,10 @@
             return jnp.minimum(jnp.abs(refs[...] - sampled), clip)
 
         term = part(window0, refs0, clip0, 1) + part(window1, refs1, clip1, 2)
-        high = term.astype(jnp.bfloat16)
-        low = (term - high.astype(jnp.float32)).astype(jnp.bfloat16)
-        terms[m * span : (m + 1) * span, 2 * p * wide : (2 * p + 1) * wide] = high
-        terms[m * span : (m + 1) * span, (2 * p + 1) * wide : (2 * p + 2) * wide] = low
+        high = (term + ROUNDER) - ROUNDER
+        here = slice(m * span, (m + 1) * span)
+        terms[here, 2 * p * wide : (2 * p + 1) * wide] = high.astype(jnp.bfloat16)
+        terms[here, (2 * p + 1) * wide : (2 * p + 2) * wide] = (term - high).astype(jnp.bfloat16)
 
     def fill(b, terms):
         for m in range(BATCH):
@@ -278,7 +274,7 @@
 
     peak = over_blocks(top[...], jnp.maximum)
     block_of = lax.broadcasted_iota(jnp.int32, (1, lanes), 1) // cols
-    part = 32
+    part = min(64, rows)
     masses, moments = [], []
     for lo in range(0, rows, part):
         high = peak[lo : lo + part]
@@ -288,7 +284,7 @@
             value = jnp.zeros((1, lanes), jnp.float32)
             for q in range(GROUP):
                 value = jnp.where(block_of == q, offs[g * GROUP + q].astype(jnp.float32), value)
-            lifted = jnp.exp(scores[g, lo : lo + part, :] - high)
+            lifted = jnp.exp2(scores[g, lo : lo + part, :] - high)
             return mass + lifted, moment + lifted * value
 
         zero = jnp.zeros((part, lanes), jnp.float32)
@@ -307,25 +303,24 @@
             dst_ref=mrx.at[i - 1],
             send_sem=msend.at[i - 1],
             recv_sem=mrecv.at[i - 1],
-            device_id={"disp": lax.rem(d + i, disp)},
+            device_id=beside(i),
         )
 
     for i in range(1, disp):
         merge_copy(i).start()
     for slot in range(back + 2):
-        for dc, imgs in each_copy(slot):
+        for dc in sides(slot):
 
             @pl.when(present(shift_of(slot), dc))
             def _():
-                for image in imgs:
-                    copy(slot, image, dc).wait_send()
+                copy(slot, dc).wait_send()
 
     peak, mass, moment = own
     for i in range(1, disp):
         merge_copy(i).wait_recv()
         other = [mrx[i - 1, k] for k in range(3)]
         new = jnp.maximum(peak, other[0])
-        mine, theirs = jnp.exp(peak - new), jnp.exp(other[0] - new)
+        mine, theirs = jnp.exp2(peak - new), jnp.exp2(other[0] - new)
         mass = mass * mine + other[1] * theirs
         moment = moment * mine + other[2] * theirs
         peak = new
@@ -369,8 +364,8 @@
             pltpu.VMEM((rows, lanes), f32),
             pltpu.VMEM((3, cols, rows), f32),
             pltpu.VMEM((max(disp - 1, 1), 3, cols, rows), f32),
-            pltpu.SemaphoreType.DMA((back + 2, 3, 3)),
-            pltpu.SemaphoreType.DMA((back + 2, 3, 3)),
+            pltpu.SemaphoreType.DMA((back + 2, 3)),
+            pltpu.SemaphoreType.DMA((back + 2, 3)),
             pltpu.SemaphoreType.DMA((max(disp - 1, 1),)),
             pltpu.SemaphoreType.DMA((max(disp - 1, 1),)),
             pltpu.SemaphoreType.DMA((5,)),
@@ -378,7 +373,7 @@
         compiler_params=pltpu.CompilerParams(collective_id=0, has_side_effects=True),
     )(plane_offsets, jnp.transpose(intersection_mask, (1, 2, 0)), ref_image, source_one, source_two)
     peak, mass, moment = merged[0], merged[1], merged[2]
-    return moment / mass / INTERVAL, -SHARPNESS * (peak + jnp.log(mass))
+    return moment / mass / INTERVAL, -SHARPNESS * (peak * LN2 + jnp.log(mass))
 
 
 def solution(mesh):

time: 19.8 us -> 18.5 us (0.934)
  Pallas kernels: 17.6 us -> 16.2 us
    pallas_call x1, Pallas kernels: 17.6 us -> 16.2 us  [shards(): pl.pallas_call(functools.partial(kernel, (track, across, disp, cols, rows...]
where the time goes in v3:
time: 18.5 us; the launch traced here: 18.2 us
  Pallas kernels  16.2 us (88%)
  other arithmetic  1.38 us (7%)
  between operations  0.64 us (3%)
    pallas_call x1, Pallas kernels, shards(): pl.pallas_call(functools.partial(kernel, (track, across, disp, cols, rows...  16.2 us
    mul x1, other arithmetic, shards(): return (moment / mass / INTERVAL, -SHARPNESS * (peak * LN2 + jnp.log(mass)))  1.38 us

profile of v3, /device:TPU:0, one launch (start us, length us, event | category | flops | bytes accessed | tf_op | source)
XLA Modules:
  0.0 18.2 jit_solution(3357185718885852856)
XLA Ops:
  0.6 16.2 %shard_map.68 = f32[3,32,128]{2,1,0:T(8,128)} custom-call(s32[128]{0:T(128)} %offs_hbm.1, s32[1,1,2]{2,1,0:T(1,128)} %bitcast.5, bf16[32,128]{1,0:T(8,128)(2,1)} %r_ref.1, bf16[32,128]{1,0:T(8,128)(2,1)} %s1_ref.1, bf16[32,128]{1,0:T(8,128)(2,1)} %s2_ref.1), custom_call_target="tpu_custom_call" | custom-call | tf_op jit(solution)/shard_map/pallas_call | solution.py:345
  16.8 1.4 %multiply_bitcast_fusion = (f32[32,128]{1,0:T(8,128)}, f32[32,128]{1,0:T(8,128)}) fusion(f32[3,32,128]{2,1,0:T(8,128)} %shard_map.68), kind=kLoop, calls=%fused_computation | loop fusion | flops 20480 | bytes 81920 | tf_op jit(solution)/shard_map/mul | solution.py:376

commit v4 on v3

--- a/solution.py
+++ b/solution.py
@@ -15,7 +15,6 @@
 INTERVAL = 64.0
 BIG = 1e30
 GROUP = 4
-ROUNDER = 1.5 * 2.0**16
 LOG2E = 1.4426950408889634
 LN2 = 0.6931471805599453
 BATCH = 4
@@ -49,7 +48,7 @@
         return (r + dr >= 0) & (r + dr < track) & (c + dc >= 0) & (c + dc < across)
 
     barrier = pltpu.get_barrier_semaphore()
-    for dr in sorted(range(-back, back + 1), key=abs, reverse=True):
+    for dr in range(-back, 2):
         for dc in (-1, 0, 1):
             if dr == 0 and dc == 0:
                 continue
@@ -68,7 +67,7 @@
     ]
     for one in local:
         one.start()
-    n_rows = jnp.minimum(r, back) + jnp.minimum(track - 1 - r, back) + 1
+    n_rows = jnp.minimum(r, 1) + jnp.minimum(track - 1 - r, back) + 1
     n_cols = jnp.minimum(c, 1) + jnp.minimum(across - 1 - c, 1) + 1
     def shift_of(slot):
         return -1 if slot == ahead else slot
@@ -218,10 +217,10 @@
             return jnp.minimum(jnp.abs(refs[...] - sampled), clip)
 
         term = part(window0, refs0, clip0, 1) + part(window1, refs1, clip1, 2)
-        high = (term + ROUNDER) - ROUNDER
+        high = term.astype(jnp.bfloat16)
         here = slice(m * span, (m + 1) * span)
-        terms[here, 2 * p * wide : (2 * p + 1) * wide] = high.astype(jnp.bfloat16)
-        terms[here, (2 * p + 1) * wide : (2 * p + 2) * wide] = (term - high).astype(jnp.bfloat16)
+        terms[here, 2 * p * wide : (2 * p + 1) * wide] = high
+        terms[here, (2 * p + 1) * wide : (2 * p + 2) * wide] = (term - high.astype(jnp.float32)).astype(jnp.bfloat16)
 
     def fill(b, terms):
         for m in range(BATCH):
@@ -288,7 +287,7 @@
             return mass + lifted, moment + lifted * value
 
         zero = jnp.zeros((part, lanes), jnp.float32)
-        mass, moment = lax.fori_loop(0, planes // GROUP, gather, (zero, zero), unroll=4)
+        mass, moment = lax.fori_loop(0, planes // GROUP, gather, (zero, zero), unroll=8)
         masses.append(mass)
         moments.append(moment)
     mass = over_blocks(jnp.concatenate(masses, axis=0), jnp.add)

time: 18.5 us -> 18.4 us (level)
  no operation moved by 1% of the time
where the time goes in v4:
time: 18.4 us; the launch traced here: 18.1 us
  Pallas kernels  16.1 us (88%)
  other arithmetic  1.38 us (8%)
  between operations  0.64 us (3%)
    pallas_call x1, Pallas kernels, shards(): pl.pallas_call(functools.partial(kernel, (track, across, disp, cols, rows...  16.1 us
    mul x1, other arithmetic, shards(): return (moment / mass / INTERVAL, -SHARPNESS * (peak * LN2 + jnp.log(mass)))  1.38 us

profile of v4, /device:TPU:0, one launch (start us, length us, event | category | flops | bytes accessed | tf_op | source)
XLA Modules:
  0.0 18.1 jit_solution(17363625766291127108)
XLA Ops:
  0.6 16.1 %shard_map.68 = f32[3,32,128]{2,1,0:T(8,128)} custom-call(s32[128]{0:T(128)} %offs_hbm.1, s32[1,1,2]{2,1,0:T(1,128)} %bitcast.5, bf16[32,128]{1,0:T(8,128)(2,1)} %r_ref.1, bf16[32,128]{1,0:T(8,128)(2,1)} %s1_ref.1, bf16[32,128]{1,0:T(8,128)(2,1)} %s2_ref.1), custom_call_target="tpu_custom_call" | custom-call | tf_op jit(solution)/shard_map/pallas_call | solution.py:344
  16.8 1.4 %multiply_bitcast_fusion = (f32[32,128]{1,0:T(8,128)}, f32[32,128]{1,0:T(8,128)}) fusion(f32[3,32,128]{2,1,0:T(8,128)} %shard_map.68), kind=kLoop, calls=%fused_computation | loop fusion | flops 20480 | bytes 81920 | tf_op jit(solution)/shard_map/mul | solution.py:375
